TPU v7x, 32 devices: a whole 2x2x4 slice. The times are simulated.
32 devices in a mesh: ch: 4 (over z), ha: 2 (over x), dp: 4 (over y, core).
Axes of the slice: x: 2, y: 2, z: 4, core: 2. Of those that a mesh axis runs over, the one named last changes fastest.
Arguments:
- features: bfloat16 [384, 4, 4, 4, 128], P('ch', 'dp', None, 'ha'), may hold values from -26 to 26
- frame_count: int32 [4], P('dp'), may hold values from 1 to 4, as said below
- norm1_gain: float32 [384], P('ch'), may hold values from 0.5 to 2
- norm1_shift: float32 [384], P('ch'), may hold values from -3 to 3
- qkv_weight: bfloat16 [384, 1152], replicated, may hold values from -0.51031036 to 0.51031036
- qkv_bias: float32 [1152], replicated, may hold values from -3 to 3
- out_weight: bfloat16 [384, 384], replicated, may hold values from -0.3125 to 0.3125
- out_bias: float32 [384], replicated, may hold values from -3 to 3
- norm2_gain: float32 [384], P('ch'), may hold values from 0.5 to 2
- norm2_shift: float32 [384], P('ch'), may hold values from -3 to 3
- conv_weight: bfloat16 [3, 3, 3, 384, 384], P(None, None, None, 'ch'), may hold values from -0.0625 to 0.0625
- conv_bias: float32 [384], P('ch'), may hold values from -3 to 3
- cotangent: bfloat16 [384, 4, 4, 4, 128], P('ch', 'dp', None, 'ha'), may hold values from -0.0625 to 0.0625
Outputs:
- mixed: bfloat16 [384, 4, 4, 4, 128], P('ch', 'dp', None, 'ha')
- weight_grad: float32 [3, 3, 3, 384, 384], P(None, None, None, 'ch')
Inputs may be any that keep to these rules, and one draw needn't show every extreme that they name: `frame_count`: some clip has all 4 frames valid and some clip only one.
All inputs are finite; a program needn't handle non-finite values.
Results may differ from a plain program's by a relative error of at most 0.015.
Values may be sent and summed in bfloat16 or wider, within the bound.
A program may use at most 64 MiB of HBM per device.

v0:
```python
import jax
import jax.numpy as jnp
from jax import lax
from jax.sharding import PartitionSpec as P

GROUPS = 32
EPS = 1e-06


def padded_2(x, sides, width):
    for axis, dim in sides:
        count, length = (lax.axis_size(axis), x.shape[dim])
        up = [(i, (i + 1) % count) for i in range(count - 1)]
        down = [(j, i) for i, j in up]
        last = lax.slice_in_dim(x, length - width, length, axis=dim)
        leading = lax.slice_in_dim(x, 0, width, axis=dim)
        before = lax.ppermute(last, axis, up)
        after = lax.ppermute(leading, axis, down)
        x = jnp.concatenate([before, x, after], axis=dim)
    return x


def frame_mask(frame_count, frames):
    position = lax.broadcasted_iota(jnp.int32, (frame_count.shape[0], frames), 1)
    return (position < frame_count[:, None]).astype(jnp.float32)


def moments(values, mask, groups):
    chans, clips, frames, rows, cols = values.shape
    data = values.astype(jnp.float32).reshape(groups, chans // groups, clips, frames, rows * cols)
    first = jnp.einsum("gkbfp,bf->gb", data, mask)
    second = jnp.einsum("gkbfp,bf->gb", data * data, mask)
    return (first, second)


def normalize(values, first, second, count, gain, shift, groups):
    chans, clips, frames, rows, cols = values.shape
    mean = first / count[None, :]
    var = second / count[None, :] - mean * mean
    scale = lax.rsqrt(var + EPS)
    data = values.astype(jnp.float32).reshape(groups, chans // groups, clips, frames, rows * cols)
    normed = (data - mean[:, None, :, None, None]) * scale[:, None, :, None, None]
    normed = normed.reshape(values.shape)
    return normed * gain[:, None, None, None, None] + shift[:, None, None, None, None]


def attend(carry, queries, keys, values, scale):
    top, total, acc = carry
    scores = jnp.einsum("itc,isc->its", queries, keys, preferred_element_type=jnp.float32) * scale
    new_top = jnp.max(scores, axis=2)
    factor = jnp.exp(top - new_top)
    weights = jnp.exp(scores - new_top[..., None])
    total = total * factor + jnp.sum(weights, axis=2)
    acc = acc * factor[..., None] + jnp.einsum(
        "its,isc->itc", weights.astype(jnp.bfloat16), values, preferred_element_type=jnp.float32
    )
    return (new_top, total, acc)


def tap_stack(padded, time_tap, frames, rows, cols):
    windows = []
    for row_tap in range(3):
        for col_tap in range(3):
            windows.append(
                padded[
                    :,
                    :,
                    time_tap : time_tap + frames,
                    row_tap : row_tap + rows,
                    col_tap : col_tap + cols,
                ]
            )
    return jnp.concatenate(windows, axis=0)


def body(
    features,
    frame_count,
    norm1_gain,
    norm1_shift,
    qkv_weight,
    qkv_bias,
    out_weight,
    out_bias,
    norm2_gain,
    norm2_shift,
    conv_weight,
    conv_bias,
    cotangent,
):
    chans, clips, frames, rows, cols = features.shape
    groups = GROUPS // lax.axis_size("ch")
    mask = frame_mask(frame_count, frames)
    count = frame_count.astype(jnp.float32) * (chans // groups * rows * lax.axis_size("ha") * cols)
    first, second = moments(features, mask, groups)
    first, second = lax.psum((first, second), "ha")
    normed = normalize(features, first, second, count, norm1_gain, norm1_shift, groups).astype(
        jnp.bfloat16
    )
    by_frame = lax.all_to_all(normed, "ch", split_axis=2, concat_axis=0, tiled=True)
    width = by_frame.shape[0]
    items = clips * by_frame.shape[2]
    tok_rows = rows * cols
    tokens = by_frame.reshape(width, items, tok_rows)
    queries = lax.dot_general(
        tokens, qkv_weight[:, :width], (((0,), (0,)), ((), ())), preferred_element_type=jnp.float32
    )
    queries = (queries + qkv_bias[:width]).astype(jnp.bfloat16)
    scale = width ** (-0.5)
    start_carry = (
        jnp.full((items, tok_rows), -jnp.inf, jnp.float32),
        jnp.zeros((items, tok_rows), jnp.float32),
        jnp.zeros((items, tok_rows, width), jnp.float32),
    )
    pairs = lax.dot_general(
        tokens, qkv_weight[:, width:], (((0,), (0,)), ((), ())), preferred_element_type=jnp.float32
    )
    pairs = (pairs + qkv_bias[width:]).astype(jnp.bfloat16)
    piece = lax.all_gather(pairs, "ha", axis=1, tiled=True)
    top, total, acc = attend(start_carry, queries, piece[..., :width], piece[..., width:], scale)
    attended = (acc / total[..., None]).astype(jnp.bfloat16)
    projected = lax.dot_general(
        out_weight, attended, (((0,), (2,)), ((), ())), preferred_element_type=jnp.float32
    )
    projected = (projected + out_bias[:, None, None]).astype(jnp.bfloat16).reshape(by_frame.shape)
    update = lax.all_to_all(projected, "ch", split_axis=0, concat_axis=2, tiled=True)
    hidden = (features.astype(jnp.float32) + update.astype(jnp.float32)).astype(jnp.bfloat16)
    first, second = moments(hidden, mask, groups)
    first, second = lax.psum((first, second), "ha")
    gated = jax.nn.silu(
        normalize(hidden, first, second, count, norm2_gain, norm2_shift, groups)
    ).astype(jnp.bfloat16)
    with_rows = padded_2(gated, (("ha", 3),), 1)
    padded = jnp.pad(with_rows, ((0, 0), (0, 0), (2, 0), (0, 0), (1, 1)))
    stacks = [tap_stack(padded, time_tap, frames, rows, cols) for time_tap in range(3)]
    amount = chans * lax.axis_size("ch")
    summed = jnp.zeros((amount, clips, frames, rows, cols), jnp.float32)
    for time_tap in range(3):
        part = conv_weight[time_tap].reshape(9 * chans, amount)
        summed = summed + lax.dot_general(
            part, stacks[time_tap], (((0,), (0,)), ((), ())), preferred_element_type=jnp.float32
        )
    conv_out = lax.psum_scatter(
        summed.astype(jnp.bfloat16), "ch", scatter_dimension=0, tiled=True
    ).astype(jnp.float32)
    mixed = mask[None, :, :, None, None] * (
        hidden.astype(jnp.float32) + conv_out + conv_bias[:, None, None, None, None]
    )
    mixed = mixed.astype(jnp.bfloat16)
    masked_cot = cotangent * mask.astype(jnp.bfloat16)[None, :, :, None, None]
    full_width = chans * lax.axis_size("ch")
    carry = jnp.zeros((3, 9 * chans, full_width), jnp.float32)
    piece = lax.all_gather(masked_cot, "ch", axis=0, tiled=True)
    start = jnp.int32(0)
    for time_tap in range(3):
        part = lax.dot_general(
            stacks[time_tap],
            piece,
            (((1, 2, 3, 4), (1, 2, 3, 4)), ((), ())),
            preferred_element_type=jnp.float32,
        )
        carry = lax.dynamic_update_slice(
            carry, part[None], (jnp.int32(time_tap), jnp.int32(0), start)
        )
    grad_table = carry
    grad_table = grad_table.reshape(3, 3, 3, chans, full_width)
    weight_grad = lax.psum(grad_table.astype(jnp.bfloat16), ("ha", "dp")).astype(jnp.float32)
    return (mixed, weight_grad)


def solution(mesh):
    placed = (
        P("ch", "dp", None, "ha", None),
        P("dp"),
        P("ch"),
        P("ch"),
        P(),
        P(),
        P(),
        P(),
        P("ch"),
        P("ch"),
        P(None, None, None, "ch", None),
        P("ch"),
        P("ch", "dp", None, "ha", None),
    )
    return jax.shard_map(
        body,
        mesh=mesh,
        in_specs=placed,
        out_specs=(P("ch", "dp", None, "ha", None), P(None, None, None, "ch", None)),
        check_vma=False,
    )
```

profile of v0, /device:TPU:0, one launch (start us, length us, event | category | flops | bytes accessed | tf_op | source)
XLA Modules:
  0.0 170.4 jit_solution(4983406673391585404)
XLA Ops:
  8.7 1.1 fusion.57
  9.8 0.1 reduce_sum.61
  10.0 0.1 reduce_sum.62
  10.1 0.1 reduce_sum.59
  10.2 0.1 convolution_bitcast_fusion.2
  10.3 0.1 convolution_bitcast_fusion.3
  10.4 5.9 %all-reduce.3 = (f32[8,1]{0,1:T(1,128)S(1)}, f32[8,1]{0,1:T(1,128)S(1)}) all-reduce(f32[8,1]{0,1:T(1,128)S(1)} %convolution_bitcast_fusion.3, f32[8,1]{0,1:T(1,128)S(1)} %convolution_bitcast_fusion.2), channel_id=1, replica_groups=mesh['ch'=4,'ha'=2,'dp'=4] {'ha'}, use_global_device_ids=true, to_apply=%region_2.0 | all-reduce | flops 16 | bytes 128 | tf_op jit(solution)/shard_map/psum | solution.py:96
  16.4 0.1 mul.117
  16.5 0.1 sub.66
  16.6 1.8 %fusion.78 = bf16[96,1,4,2,128]{4,0,3,1,2:T(8,128)(2,1)} fusion(f32[96]{0:T(128)} %param.16, f32[96]{0:T(128)} %param.15, f32[96]{0:T(128)S(1)} %mul.117, f32[96]{0:T(128)S(1)} %sub.66, bf16[96,1,4,2,128]{4,3,2,1,0:T(2,128)(2,1)} %param.13), kind=kLoop, calls=%fused_computation.84 | loop fusion | flops 589824 | bytes 394752 | tf_op jit(solution)/shard_map/convert_element_type | solution.py:97
  18.4 5.5 %all-to-all-start = ((bf16[96,1,4,2,128]{4,0,3,1,2:T(8,128)(2,1)}), bf16[96,1,4,2,128]{4,0,3,1,2:T(8,128)(2,1)S(1)}, u32[]{:S(2)}, u32[]{:S(2)}) async-start(bf16[96,1,4,2,128]{4,0,3,1,2:T(8,128)(2,1)} %fusion.78), calls=%async_computation | async-start | bytes 393216 | tf_op jit(solution)/shard_map/all_to_all | solution.py:100
  24.0 0.7 slice.120
  24.7 5.5 %all-to-all-done = bf16[96,1,4,2,128]{4,0,3,1,2:T(8,128)(2,1)S(1)} async-done(((bf16[96,1,4,2,128]{4,0,3,1,2:T(8,128)(2,1)}), bf16[96,1,4,2,128]{4,0,3,1,2:T(8,128)(2,1)S(1)}, u32[]{:S(2)}, u32[]{:S(2)}) %all-to-all-start) | async-done | bytes 196640 | tf_op jit(solution)/shard_map/all_to_all | solution.py:100
  30.2 0.2 copy.32
  30.4 1.5 fusion.37
  31.8 8.9 %all-gather = bf16[512,768]{1,0:T(8,128)(2,1)S(1)} all-gather(bf16[256,768]{1,0:T(8,128)(2,1)S(1)} %fusion.37), channel_id=2, replica_groups=mesh['ch'=4,'ha'=2,'dp'=4] {'ha'}, dimensions={0}, use_global_device_ids=true | all-gather | bytes 1179648 | tf_op jit(solution)/shard_map/all_gather | solution.py:119
  40.8 1.6 fusion.104
  42.4 0.2 fusion.51
  42.7 0.6 fusion.46
  43.3 0.9 copy.33
  44.1 3.5 %all-to-all-start.1 = ((bf16[384,1,1,2,128]{4,3,2,1,0:T(2,128)(2,1)}), bf16[384,1,1,2,128]{4,3,2,1,0:T(2,128)(2,1)S(1)}, u32[]{:S(2)}, u32[]{:S(2)}) async-start(bf16[384,1,1,2,128]{4,3,2,1,0:T(2,128)(2,1)} %copy.33), calls=%async_computation.1 | async-start | bytes 393216 | tf_op jit(solution)/shard_map/all_to_all | solution.py:126
  47.7 0.1 copy_multiply_fusion
  47.8 6.1 %all-to-all-done.1 = bf16[384,1,1,2,128]{4,3,2,1,0:T(2,128)(2,1)S(1)} async-done(((bf16[384,1,1,2,128]{4,3,2,1,0:T(2,128)(2,1)}), bf16[384,1,1,2,128]{4,3,2,1,0:T(2,128)(2,1)S(1)}, u32[]{:S(2)}, u32[]{:S(2)}) %all-to-all-start.1) | async-done | bytes 196640 | tf_op jit(solution)/shard_map/all_to_all | solution.py:126
  54.0 0.2 fusion.68
  54.3 0.1 reduce_sum.85
  54.4 0.1 reduce_sum.82
  54.5 0.1 convolution_bitcast_fusion
  54.6 0.1 convolution_bitcast_fusion.1
  54.8 17.3 %all_gather.7 = bf16[384,1,4,2,128]{4,0,3,2,1:T(8,128)(2,1)} all-gather(bf16[96,1,4,2,128]{4,0,3,2,1:T(8,128)(2,1)S(1)} %copy_multiply_fusion), channel_id=1, replica_groups=mesh['ch'=4,'ha'=2,'dp'=4] {'ch'}, dimensions={0}, use_global_device_ids=true | all-gather | bytes 983040 | tf_op jit(solution)/shard_map/all_gather | solution.py:153
  72.1 4.9 %all-reduce.2 = (f32[8,1]{0,1:T(1,128)S(1)}, f32[8,1]{0,1:T(1,128)S(1)}) all-reduce(f32[8,1]{0,1:T(1,128)S(1)} %convolution_bitcast_fusion.1, f32[8,1]{0,1:T(1,128)S(1)} %convolution_bitcast_fusion), channel_id=1, replica_groups=mesh['ch'=4,'ha'=2,'dp'=4] {'ha'}, use_global_device_ids=true, to_apply=%region_10.11 | all-reduce | flops 16 | bytes 128 | tf_op jit(solution)/shard_map/psum | solution.py:129
  77.1 0.1 mul.129
  77.2 0.1 sub.75
  77.3 0.3 fusion.67
  77.7 3.4 %collective-permute-start = (bf16[96,1,4,1,128]{4,0,3,2,1:T(8,128)(2,1)S(1)}, bf16[96,1,4,1,128]{4,0,3,2,1:T(8,128)(2,1)S(1)}, u32[]{:S(2)}, u32[]{:S(2)}) collective-permute-start(bf16[96,1,4,1,128]{4,0,3,2,1:T(8,128)(2,1)S(1)} %get-tuple-element.47), channel_id=1, source_target_pairs={{0,4},{1,5},{2,6},{3,7},{8,12},{9,13},{10,14},{11,15},{16,20},{17,... | collective-permute-start | bytes 294920 | tf_op jit(solution)/shard_map/ppermute | solution.py:17
  81.1 1.3 collective-permute-start.1
  82.4 1.3 fusion.102
  83.7 3.9 %collective-permute-done.1 = bf16[96,1,4,1,128]{4,0,3,2,1:T(8,128)(2,1)S(1)} collective-permute-done((bf16[96,1,4,1,128]{4,0,3,2,1:T(8,128)(2,1)S(1)}, bf16[96,1,4,1,128]{4,0,3,2,1:T(8,128)(2,1)S(1)}, u32[]{:S(2)}, u32[]{:S(2)}) %collective-permute-start.1) | collective-permute-done | bytes 98336 | tf_op jit(solution)/shard_map/ppermute | solution.py:18
  87.6 0.4 fusion.41
  88.1 0.2 slice_dynamic-update-slice_fusion.13
  88.3 0.2 slice_dynamic-update-slice_fusion.12
  88.5 0.1 slice_dynamic-update-slice_fusion.11
  88.6 0.2 slice_dynamic-update-slice_fusion.10
  88.9 0.3 slice_dynamic-update-slice_fusion.9
  89.2 0.1 slice_dynamic-update-slice_fusion.8
  89.4 0.4 constant_dynamic-update-slice_fusion
  89.8 0.3 slice_dynamic-update-slice_fusion.7
  90.1 0.3 slice_dynamic-update-slice_fusion.6
  90.4 1.1 fusion.19
  91.5 0.1 copy-done.10
  91.6 0.2 dynamic_update_slice.9
  91.8 0.1 slice_dynamic-update-slice_fusion
  91.9 0.2 copy-done.9
  92.1 1.2 fusion.25
  93.3 1.2 fusion.31
  94.5 1.3 copy-done.1
  95.8 0.2 reduce-scatter.2.cloned.1.call-start
  96.1 2.8 %fusion.11 = f32[4,2,128,384]{2,3,1,0:T(8,128)S(1)} fusion(bf16[864,384,1,1]{1,0,3,2:T(8,128)(2,1)} %bitcast.175, bf16[864,1,4,2,128]{4,0,3,2,1:T(8,128)(2,1)} %copy-done.9), kind=kOutput, calls=%fused_computation.14 | convolution fusion | flops 679477248 | bytes 4005888 | tf_op jit(solution)/shard_map/dot_general | solution.py:140
  98.9 1.0 fusion.15
  100.0 0.4 copy-done.3
  100.4 2.0 %fusion.34 = bf16[384,1,4,2,128]{4,0,3,2,1:T(8,128)(2,1)} fusion(bf16[864,384,1,1]{1,0,3,2:T(8,128)(2,1)S(1)} %bitcast.169, bf16[864,1,4,2,128]{4,0,3,2,1:T(8,128)(2,1)S(1)} %copy-done.3, f32[4,2,128,384]{2,3,1,0:T(8,128)S(1)} %fusion.15, f32[4,2,128,384]{2,3,1,0:T(8,128)S(1)} %fusion.11), kind=kOutput, calls=%fused_computation.26 | convolution fusion | flops 680656896 | bytes 6365184 | tf_op jit(solution)/shard_map/dot_general | solution.py:140
  102.4 54.7 %all-reduce.6.cloned.1.call-done = bf16[3,3,3,96,384]{4,3,2,1,0:T(8,128)(2,1)} async-done(((bf16[3,3,3,96,384]{4,3,2,1,0:T(8,128)(2,1)}), bf16[3,3,3,96,384]{4,3,2,1,0:T(8,128)(2,1)}) %all-reduce.6.cloned.1.call-update) | async-done | bytes 1990672 | tf_op jit(solution)/shard_map/psum | solution.py:167
  157.1 4.0 %convert_element_type.145 = f32[3,3,3,96,384]{4,3,2,1,0:T(8,128)} convert(bf16[3,3,3,96,384]{4,3,2,1,0:T(8,128)(2,1)} %all-reduce.6.cloned.1.call-done) | non-fusion elementwise | flops 995328 | bytes 5971968 | tf_op jit(solution)/shard_map/convert_element_type | solution.py:167
  161.1 1.1 fusion.71
  162.1 0.8 copy.40
  (52 shorter events, 0.9 us)
Async XLA Ops:
  8.0 34.6 %copy-start = (bf16[384,384]{1,0:T(8,128)(2,1)S(1)}, bf16[384,384]{1,0:T(8,128)(2,1)}, u32[]{:S(2)}) copy-start(bf16[384,384]{1,0:T(8,128)(2,1)} %param.19) | copy-start | bytes 884740
  18.4 22.4 %slice-start = ((f32[1152]{0:T(1024)}), f32[384]{0:T(512)S(1)}, s32[]{:S(2)}) async-start(f32[1152]{0:T(1024)} %param.18), calls=%async_computation.5 | async-start | bytes 4096 | tf_op jit(solution)/shard_map/slice | solution.py:108
  18.4 11.8 %all-to-all-start = ((bf16[96,1,4,2,128]{4,0,3,1,2:T(8,128)(2,1)}), bf16[96,1,4,2,128]{4,0,3,1,2:T(8,128)(2,1)S(1)}, u32[]{:S(2)}, u32[]{:S(2)}) async-start(bf16[96,1,4,2,128]{4,0,3,1,2:T(8,128)(2,1)} %fusion.78), calls=%async_computation | async-start | bytes 393216 | tf_op jit(solution)/shard_map/all_to_all | solution.py:100
  31.8 10.8 %copy-start.15 = (f32[384]{0:T(512)S(1)}, f32[384]{0:T(512)}, u32[]{:S(2)}) copy-start(f32[384]{0:T(512)} %param.20) | copy-start | bytes 4612
  42.6 5.1 %copy-start.8 = (bf16[96,1,4,2,128]{4,3,2,1,0:T(2,128)(2,1)S(1)}, bf16[96,1,4,2,128]{4,3,2,1,0:T(2,128)(2,1)}, u32[]{:S(2)}) copy-start(bf16[96,1,4,2,128]{4,3,2,1,0:T(2,128)(2,1)} %param.25) | copy-start | bytes 589828
  42.6 11.3 %copy-start.5 = (bf16[96,1,4,2,128]{4,3,2,1,0:T(2,128)(2,1)S(1)}, bf16[96,1,4,2,128]{4,3,2,1,0:T(2,128)(2,1)}, u32[]{:S(2)}) copy-start(bf16[96,1,4,2,128]{4,3,2,1,0:T(2,128)(2,1)} %param.13) | copy-start | bytes 589828
  43.2 34.1 %copy-start.12 = (f32[96]{0:T(128)S(1)}, f32[96]{0:T(128)}, u32[]{:S(2)}) copy-start(f32[96]{0:T(128)} %param.22) | copy-start | bytes 1156
  43.3 34.1 %copy-start.13 = (f32[96]{0:T(128)S(1)}, f32[96]{0:T(128)}, u32[]{:S(2)}) copy-start(f32[96]{0:T(128)} %param.21) | copy-start | bytes 1156
  44.1 38.3 %copy-start.4 = (bf16[3,3,3,96,384]{4,3,2,1,0:T(8,128)(2,1)S(1)}, bf16[3,3,3,96,384]{4,3,2,1,0:T(8,128)(2,1)}, u32[]{:S(2)}) copy-start(bf16[3,3,3,96,384]{4,3,2,1,0:T(8,128)(2,1)} %param.23) | copy-start | bytes 5971972
  44.1 9.8 %all-to-all-start.1 = ((bf16[384,1,1,2,128]{4,3,2,1,0:T(2,128)(2,1)}), bf16[384,1,1,2,128]{4,3,2,1,0:T(2,128)(2,1)S(1)}, u32[]{:S(2)}, u32[]{:S(2)}) async-start(bf16[384,1,1,2,128]{4,3,2,1,0:T(2,128)(2,1)} %copy.33), calls=%async_computation.1 | async-start | bytes 393216 | tf_op jit(solution)/shard_map/all_to_all | solution.py:126
  47.6 109.4 %all-reduce.6.cloned.1.call-start = ((), (), s32[]{:S(2)}) async-start(), calls=%async_computation.4 | async-start | bytes 3981312 | tf_op jit(solution)/shard_map/psum | solution.py:167
  77.7 6.1 %collective-permute-start = (bf16[96,1,4,1,128]{4,0,3,2,1:T(8,128)(2,1)S(1)}, bf16[96,1,4,1,128]{4,0,3,2,1:T(8,128)(2,1)S(1)}, u32[]{:S(2)}, u32[]{:S(2)}) collective-permute-start(bf16[96,1,4,1,128]{4,0,3,2,1:T(8,128)(2,1)S(1)} %get-tuple-element.47), channel_id=1, source_target_pairs={{0,4},{1,5},{2,6},{3,7},{8,12},{9,13},{10,14},{11,15},{16,20},{17,... | collective-permute-start | bytes 294920 | tf_op jit(solution)/shard_map/ppermute | solution.py:17
  81.1 6.5 %collective-permute-start.1 = (bf16[96,1,4,1,128]{4,0,3,2,1:T(8,128)(2,1)S(1)}, bf16[96,1,4,1,128]{4,0,3,2,1:T(8,128)(2,1)S(1)}, u32[]{:S(2)}, u32[]{:S(2)}) collective-permute-start(bf16[96,1,4,1,128]{4,0,3,2,1:T(8,128)(2,1)S(1)} %get-tuple-element.48), channel_id=1, source_target_pairs={{4,0},{5,1},{6,2},{7,3},{12,8},{13,9},{14,10},{15,11},{20,16},{21,... | collective-permute-start | bytes 294920 | tf_op jit(solution)/shard_map/ppermute | solution.py:18
  89.2 1.1 copy-start.6
  90.3 1.2 copy-start.10
  90.3 1.8 %copy-start.9 = (bf16[864,1,4,2,128]{4,0,3,2,1:T(8,128)(2,1)}, bf16[864,1,4,2,128]{4,0,3,2,1:T(8,128)(2,1)S(1)}, u32[]{:S(2)}) copy-start(bf16[864,1,4,2,128]{4,0,3,2,1:T(8,128)(2,1)S(1)} %get-tuple-element.24) | copy-start | bytes 5308420
  91.9 1.4 copy-start.2
  94.5 1.3 copy-start.1
  95.8 65.2 %reduce-scatter.2.cloned.1.call-start = ((), (), s32[]{:S(2)}) async-start(), calls=%async_computation.3 | async-start | bytes 983040 | tf_op jit(solution)/shard_map/reduce_scatter | solution.py:143
  96.1 2.8 %copy-start.7 = (bf16[1,3,3,96,384]{4,3,2,1,0:T(8,128)(2,1)S(1)}, bf16[1,3,3,96,384]{4,3,2,1,0:T(8,128)(2,1)}, u32[]{:S(2)}) copy-start(bf16[1,3,3,96,384]{4,3,2,1,0:T(8,128)(2,1)} %get-tuple-element.22) | copy-start | bytes 1990660
  96.1 2.8 %copy-start.11 = (bf16[864,1,4,2,128]{4,0,3,2,1:T(8,128)(2,1)S(1)}, bf16[864,1,4,2,128]{4,0,3,2,1:T(8,128)(2,1)}, u32[]{:S(2)}) copy-start(bf16[864,1,4,2,128]{4,0,3,2,1:T(8,128)(2,1)} %copy-done.10) | copy-start | bytes 5308420
  98.9 1.5 copy-start.3
  102.4 58.7 %copy-start.14 = (f32[96]{0:T(128)S(1)}, f32[96]{0:T(128)}, u32[]{:S(2)}) copy-start(f32[96]{0:T(128)} %param.24) | copy-start | bytes 1156
Sparse Core Ops, SparseCore 0:
  96.0 61.0 all-reduce.5
Sparse Core Ops, SparseCore 1:
  102.5 22.9 reduce-scatter.1
where the time goes:
time: 171 us; the launch traced here: 170 us
  waiting for transfers between devices  70.3 us (41%)
  blocking collectives  37 us (22%)
  between operations  16.6 us (10%)
  starting transfers between devices  14 us (8%)
  matrix products  13.4 us (8%)
  other arithmetic  10.1 us (6%)
  local copies, waits for them, and re-layouts  9.05 us (5%)
    psum x1, waiting for transfers between devices, body(): lax.psum(grad_table.astype(jnp.bfloat16), ('ha', 'dp')).astype(jnp.float32)  54.7 us
    all_gather x1, blocking collectives, body(): piece = lax.all_gather(masked_cot, 'ch', axis=0, tiled=True)  17.3 us
    psum x2, blocking collectives, body(): first, second = lax.psum((first, second), 'ha')  10.8 us
    all_gather x1, blocking collectives, body(): piece = lax.all_gather(pairs, 'ha', axis=1, tiled=True)  8.94 us
    all_to_all x1, waiting for transfers between devices, body(): lax.all_to_all(projected, 'ch', split_axis=0, concat_axis=2, tiled=True)  6.12 us
    dot_general x3, matrix products, body(): lax.dot_general(part, stacks[time_tap], (((0,), (0,)), ((), ())), preferr...  5.78 us
    all_to_all x1, waiting for transfers between devices, body(): lax.all_to_all(normed, 'ch', split_axis=2, concat_axis=0, tiled=True)  5.55 us
    all_to_all x1, starting transfers between devices, body(): lax.all_to_all(normed, 'ch', split_axis=2, concat_axis=0, tiled=True)  5.54 us
  transfers between devices with their start and end apart: 6, of which 4 were waited for; matrix products, arithmetic and copies ran while one was open for 7% of the time, Pallas kernels for 0%

commit v1 on v0

--- a/solution.py
+++ b/solution.py
@@ -150,7 +150,17 @@
     masked_cot = cotangent * mask.astype(jnp.bfloat16)[None, :, :, None, None]
     full_width = chans * lax.axis_size("ch")
     carry = jnp.zeros((3, 9 * chans, full_width), jnp.float32)
-    piece = lax.all_gather(masked_cot, "ch", axis=0, tiled=True)
+    devices, here, span = (lax.axis_size("ch"), lax.axis_index("ch"), masked_cot.shape[0])
+    forward = [(i_2, (i_2 + 1) % devices) for i_2 in range(devices)]
+    piece = jnp.zeros(
+        (*masked_cot.shape[:0], devices * span, *masked_cot.shape[0 + 1 :]), masked_cot.dtype
+    )
+    held = masked_cot
+    for step in range(devices):
+        owner = (here - step) % devices
+        piece = lax.dynamic_update_slice_in_dim(piece, held, owner * span, axis=0)
+        if step < devices - 1:
+            held = lax.ppermute(held, "ch", forward)
     start = jnp.int32(0)
     for time_tap in range(3):
         part = lax.dot_general(

time: 171 us -> 160 us (0.936)
  blocking collectives: 37 us -> 19.6 us
  starting transfers between devices: 14 us -> 18.7 us
  local copies, waits for them, and re-layouts: 9.05 us -> 12.7 us
  waiting for transfers between devices: 70.3 us -> 67.5 us
    all_gather x1 -> x0, blocking collectives: 17.3 us -> none  [body(): piece = lax.all_gather(masked_cot, 'ch', axis=0, tiled=True)]
    all_to_all x1, waiting for transfers between devices: 5.55 us -> 0.42 us  [body(): lax.all_to_all(normed, 'ch', split_axis=2, concat_axis=0, tiled=True)]
    ppermute x0 -> x3, waiting for transfers between devices: none -> 3.86 us  [body(): held = lax.ppermute(held, 'ch', forward)]
    ppermute x0 -> x3, starting transfers between devices: none -> 3.81 us  [body(): held = lax.ppermute(held, 'ch', forward)]
    dynamic_update_slice x0 -> x4, local copies, waits for them, and re-layouts: none -> 2.07 us  [body(): piece = lax.dynamic_update_slice_in_dim(piece, held, owner * span, axis=0)]
    all_to_all x1, waiting for transfers between devices: 6.12 us -> 4.28 us  [body(): lax.all_to_all(projected, 'ch', split_axis=0, concat_axis=2, tiled=True)]
    unnamed x41 -> x45, local copies, waits for them, and re-layouts: 4.48 us -> 5.13 us
  transfers between devices with their start and end apart: 6 -> 9, of which waited for: 4 -> 6; matrix products, arithmetic and copies ran while one was open for 7% -> 13% of each run, Pallas kernels for 0% -> 0%
where the time goes in v1:
time: 160 us; the launch traced here: 159 us
  waiting for transfers between devices  67.5 us (42%)
  blocking collectives  19.6 us (12%)
  starting transfers between devices  18.7 us (12%)
  between operations  16.7 us (10%)
  local copies, waits for them, and re-layouts  12.7 us (8%)
  matrix products  12.2 us (8%)
  other arithmetic  11.4 us (7%)
    psum x1, waiting for transfers between devices, body(): lax.psum(grad_table.astype(jnp.bfloat16), ('ha', 'dp')).astype(jnp.float32)  53.8 us
    psum x2, blocking collectives, body(): first, second = lax.psum((first, second), 'ha')  10.8 us
    all_gather x1, blocking collectives, body(): piece = lax.all_gather(pairs, 'ha', axis=1, tiled=True)  8.81 us
    dot_general x3, matrix products, body(): lax.dot_general(part, stacks[time_tap], (((0,), (0,)), ((), ())), preferr...  5.73 us
    all_to_all x1, starting transfers between devices, body(): lax.all_to_all(normed, 'ch', split_axis=2, concat_axis=0, tiled=True)  5.41 us
    unnamed x45, local copies, waits for them, and re-layouts  5.13 us
    all_to_all x1, starting transfers between devices, body(): lax.all_to_all(projected, 'ch', split_axis=0, concat_axis=2, tiled=True)  4.52 us
    ppermute x1, waiting for transfers between devices, padded_2(): after = lax.ppermute(leading, axis, down)  4.32 us
  transfers between devices with their start and end apart: 9, of which 6 were waited for; matrix products, arithmetic and copies ran while one was open for 13% of the time, Pallas kernels for 0%

profile of v1, /device:TPU:0, one launch (start us, length us, event | category | flops | bytes accessed | tf_op | source)
XLA Modules:
  0.0 158.9 jit_solution(13526674115543186285)
XLA Ops:
  8.7 1.1 fusion.54
  10.0 0.1 reduce_sum.62
  10.2 0.1 convolution_bitcast_fusion.2
  10.3 0.1 convolution_bitcast_fusion.3
  10.4 5.9 %all-reduce.3 = (f32[8,1]{0,1:T(1,128)S(1)}, f32[8,1]{0,1:T(1,128)S(1)}) all-reduce(f32[8,1]{0,1:T(1,128)S(1)} %convolution_bitcast_fusion.3, f32[8,1]{0,1:T(1,128)S(1)} %convolution_bitcast_fusion.2), channel_id=1, replica_groups=mesh['ch'=4,'ha'=2,'dp'=4] {'ha'}, use_global_device_ids=true, to_apply=%region_2.0 | all-reduce | flops 16 | bytes 128 | tf_op jit(solution)/shard_map/psum | solution.py:96
  16.6 1.8 %fusion.75 = bf16[96,1,4,2,128]{4,0,3,1,2:T(8,128)(2,1)} fusion(f32[96]{0:T(128)} %param.16, f32[96]{0:T(128)} %param.15, f32[96]{0:T(128)S(1)} %mul.129, f32[96]{0:T(128)S(1)} %sub.75, bf16[96,1,4,2,128]{4,3,2,1,0:T(2,128)(2,1)} %param.13), kind=kLoop, calls=%fused_computation.81 | loop fusion | flops 589824 | bytes 394752 | tf_op jit(solution)/shard_map/convert_element_type | solution.py:97
  18.4 5.4 %all-to-all-start = ((bf16[96,1,4,2,128]{4,0,3,1,2:T(8,128)(2,1)}), bf16[96,1,4,2,128]{4,0,3,1,2:T(8,128)(2,1)S(1)}, u32[]{:S(2)}, u32[]{:S(2)}) async-start(bf16[96,1,4,2,128]{4,0,3,1,2:T(8,128)(2,1)} %fusion.75), calls=%async_computation | async-start | bytes 393216 | tf_op jit(solution)/shard_map/all_to_all | solution.py:100
  23.8 1.2 broadcast_multiply_fusion
  25.0 2.1 %collective-permute-start.2 = (bf16[96,1,4,2,128]{4,3,2,1,0:T(2,128)(2,1)S(1)}, bf16[96,1,4,2,128]{4,3,2,1,0:T(2,128)(2,1)}, u32[]{:S(2)}, u32[]{:S(2)}) collective-permute-start(bf16[96,1,4,2,128]{4,3,2,1,0:T(2,128)(2,1)S(1)} %broadcast_multiply_fusion), channel_id=1, source_target_pairs={{0,8},{8,16},{16,24},{24,0},{1,9},{9,17},{17,25},{25,1},{2,10},{10... | collective-permute-start | bytes 589832 | tf_op jit(solution)/shard_map/ppermute | solution.py:163
  27.1 2.8 %fusion.99 = (bf16[1,3,3,96,384]{4,3,2,1,0:T(8,128)(2,1)}, bf16[1,3,3,96,384]{4,3,2,1,0:T(8,128)(2,1)}, bf16[1,3,3,96,384]{4,3,2,1,0:T(8,128)(2,1)S(1)}) fusion(bf16[3,3,3,96,384]{4,3,2,1,0:T(8,128)(2,1)} %param.23), kind=kLoop, calls=%fused_computation.142 | loop fusion | bytes 3981312 | tf_op jit(solution)/shard_map/slice | solution.py:139
  29.9 0.2 fusion.117
  30.3 0.1 broadcast.128
  30.5 3.9 %collective-permute-done.2 = bf16[96,1,4,2,128]{4,3,2,1,0:T(2,128)(2,1)} collective-permute-done((bf16[96,1,4,2,128]{4,3,2,1,0:T(2,128)(2,1)S(1)}, bf16[96,1,4,2,128]{4,3,2,1,0:T(2,128)(2,1)}, u32[]{:S(2)}, u32[]{:S(2)}) %collective-permute-start.2) | collective-permute-done | bytes 196640 | tf_op jit(solution)/shard_map/ppermute | solution.py:163
  34.3 0.4 all-to-all-done
  34.7 0.2 copy.38
  34.9 0.4 fusion.37
  35.3 8.8 %all-gather = bf16[512,768]{1,0:T(8,128)(2,1)S(1)} all-gather(bf16[256,768]{1,0:T(8,128)(2,1)S(1)} %fusion.37), channel_id=2, replica_groups=mesh['ch'=4,'ha'=2,'dp'=4] {'ha'}, dimensions={0}, use_global_device_ids=true | all-gather | bytes 1179648 | tf_op jit(solution)/shard_map/all_gather | solution.py:119
  44.1 1.6 %fusion.101 = (f32[256]{0:T(256)S(1)}, f32[256,512]{1,0:T(8,128)S(1)}) fusion(bf16[1,512,768]{2,1,0:T(8,128)(2,1)S(1)} %bitcast.171, bf16[384,1152]{1,0:T(8,128)(2,1)} %param.17, f32[384]{0:T(512)S(1)} %slice-done, bf16[48,8,2,128]{3,2,1,0:T(2,128)(2,1)S(1)} %bitcast.179), kind=kOutput, calls=%fused_computation.144 | convolution fusion | flops 176619264 | bytes 1412096 | tf_op jit(solution)/shard_map/itc,isc->its/dot_general | solution.py:49
  45.7 0.2 fusion.48
  46.0 0.6 fusion.46
  46.6 0.9 copy.39
  47.4 4.5 %all-to-all-start.1 = ((bf16[384,1,1,2,128]{4,3,2,1,0:T(2,128)(2,1)}), bf16[384,1,1,2,128]{4,3,2,1,0:T(2,128)(2,1)S(1)}, u32[]{:S(2)}, u32[]{:S(2)}) async-start(bf16[384,1,1,2,128]{4,3,2,1,0:T(2,128)(2,1)} %copy.39), calls=%async_computation.1 | async-start | bytes 393216 | tf_op jit(solution)/shard_map/all_to_all | solution.py:126
  52.0 1.0 copy_dynamic-update-slice_fusion.2
  53.0 1.0 copy_dynamic-update-slice_fusion.1
  53.9 4.3 %all-to-all-done.1 = bf16[384,1,1,2,128]{4,3,2,1,0:T(2,128)(2,1)S(1)} async-done(((bf16[384,1,1,2,128]{4,3,2,1,0:T(2,128)(2,1)}), bf16[384,1,1,2,128]{4,3,2,1,0:T(2,128)(2,1)S(1)}, u32[]{:S(2)}, u32[]{:S(2)}) %all-to-all-start.1) | async-done | bytes 196640 | tf_op jit(solution)/shard_map/all_to_all | solution.py:126
  58.3 0.2 fusion.65
  58.6 0.1 reduce_sum.85
  58.7 0.1 reduce_sum.82
  58.8 0.1 convolution_bitcast_fusion
  59.0 0.1 convolution_bitcast_fusion.1
  59.1 1.7 %collective-permute-start.4 = (bf16[96,1,4,2,128]{4,3,2,1,0:T(2,128)(2,1)}, bf16[96,1,4,2,128]{4,3,2,1,0:T(2,128)(2,1)S(1)}, u32[]{:S(2)}, u32[]{:S(2)}) collective-permute-start(bf16[96,1,4,2,128]{4,3,2,1,0:T(2,128)(2,1)} %collective-permute-done.3), channel_id=1, source_target_pairs={{0,8},{8,16},{16,24},{24,0},{1,9},{9,17},{17,25},{25,1},{2,10},{10... | collective-permute-start | bytes 589832 | tf_op jit(solution)/shard_map/ppermute | solution.py:163
  60.8 4.9 %all-reduce.2 = (f32[8,1]{0,1:T(1,128)S(1)}, f32[8,1]{0,1:T(1,128)S(1)}) all-reduce(f32[8,1]{0,1:T(1,128)S(1)} %convolution_bitcast_fusion.1, f32[8,1]{0,1:T(1,128)S(1)} %convolution_bitcast_fusion), channel_id=1, replica_groups=mesh['ch'=4,'ha'=2,'dp'=4] {'ha'}, use_global_device_ids=true, to_apply=%region_10.11 | all-reduce | flops 16 | bytes 128 | tf_op jit(solution)/shard_map/psum | solution.py:129
  66.0 0.3 fusion.64
  66.4 3.4 %collective-permute-start = (bf16[96,1,4,1,128]{4,0,3,2,1:T(8,128)(2,1)S(1)}, bf16[96,1,4,1,128]{4,0,3,2,1:T(8,128)(2,1)S(1)}, u32[]{:S(2)}, u32[]{:S(2)}) collective-permute-start(bf16[96,1,4,1,128]{4,0,3,2,1:T(8,128)(2,1)S(1)} %get-tuple-element.47), channel_id=1, source_target_pairs={{0,4},{1,5},{2,6},{3,7},{8,12},{9,13},{10,14},{11,15},{16,20},{17,... | collective-permute-start | bytes 294920 | tf_op jit(solution)/shard_map/ppermute | solution.py:17
  69.8 1.3 collective-permute-start.1
  71.2 0.8 collective-permute-done
  72.0 4.3 %collective-permute-done.1 = bf16[96,1,4,1,128]{4,0,3,2,1:T(8,128)(2,1)S(1)} collective-permute-done((bf16[96,1,4,1,128]{4,0,3,2,1:T(8,128)(2,1)S(1)}, bf16[96,1,4,1,128]{4,0,3,2,1:T(8,128)(2,1)S(1)}, u32[]{:S(2)}, u32[]{:S(2)}) %collective-permute-start.1) | collective-permute-done | bytes 98336 | tf_op jit(solution)/shard_map/ppermute | solution.py:18
  76.3 0.4 fusion.41
  76.8 0.2 slice_dynamic-update-slice_fusion.13
  77.0 0.2 slice_dynamic-update-slice_fusion.12
  77.3 0.1 slice_dynamic-update-slice_fusion.11
  77.4 0.3 slice_dynamic-update-slice_fusion.10
  77.6 0.3 slice_dynamic-update-slice_fusion.9
  78.0 0.1 slice_dynamic-update-slice_fusion.8
  78.1 0.4 constant_dynamic-update-slice_fusion
  78.5 0.3 slice_dynamic-update-slice_fusion.7
  78.8 0.3 slice_dynamic-update-slice_fusion.6
  79.1 1.1 fusion.19
  80.3 0.2 dynamic_update_slice.29
  80.5 0.1 slice_dynamic-update-slice_fusion
  80.7 0.2 copy-done.9
  80.9 0.6 copy-done.7
  81.4 1.2 fusion.25
  82.6 1.2 fusion.31
  83.8 1.3 copy-done.1
  85.1 0.2 reduce-scatter.2.cloned.1.call-start
  85.4 2.8 %fusion.11 = f32[4,2,128,384]{2,3,1,0:T(8,128)S(1)} fusion(bf16[864,384,1,1]{1,0,3,2:T(8,128)(2,1)} %bitcast.176, bf16[864,1,4,2,128]{4,0,3,2,1:T(8,128)(2,1)} %copy-done.9), kind=kOutput, calls=%fused_computation.14 | convolution fusion | flops 679477248 | bytes 4005888 | tf_op jit(solution)/shard_map/dot_general | solution.py:140
  88.2 1.0 fusion.15
  89.2 0.5 copy-done.3
  89.7 1.9 %fusion.34 = bf16[384,1,4,2,128]{4,0,3,2,1:T(8,128)(2,1)} fusion(bf16[864,384,1,1]{1,0,3,2:T(8,128)(2,1)S(1)} %bitcast.170, bf16[864,1,4,2,128]{4,0,3,2,1:T(8,128)(2,1)S(1)} %copy-done.3, f32[4,2,128,384]{2,3,1,0:T(8,128)S(1)} %fusion.15, f32[4,2,128,384]{2,3,1,0:T(8,128)S(1)} %fusion.11), kind=kOutput, calls=%fused_computation.26 | convolution fusion | flops 680656896 | bytes 6365184 | tf_op jit(solution)/shard_map/dot_general | solution.py:140
  91.7 53.8 %all-reduce.6.cloned.1.call-done = bf16[3,3,3,96,384]{4,3,2,1,0:T(8,128)(2,1)} async-done(((bf16[3,3,3,96,384]{4,3,2,1,0:T(8,128)(2,1)}), bf16[3,3,3,96,384]{4,3,2,1,0:T(8,128)(2,1)}) %all-reduce.6.cloned.1.call-update) | async-done | bytes 1990672 | tf_op jit(solution)/shard_map/psum | solution.py:177
  145.5 4.0 %convert_element_type.145 = f32[3,3,3,96,384]{4,3,2,1,0:T(8,128)} convert(bf16[3,3,3,96,384]{4,3,2,1,0:T(8,128)(2,1)} %all-reduce.6.cloned.1.call-done) | non-fusion elementwise | flops 995328 | bytes 5971968 | tf_op jit(solution)/shard_map/convert_element_type | solution.py:177
  149.5 1.1 fusion.68
  150.6 0.8 copy.49
  (67 shorter events, 1.5 us)
Async XLA Ops:
  8.0 38.0 %copy-start = (bf16[384,384]{1,0:T(8,128)(2,1)S(1)}, bf16[384,384]{1,0:T(8,128)(2,1)}, u32[]{:S(2)}) copy-start(bf16[384,384]{1,0:T(8,128)(2,1)} %param.19) | copy-start | bytes 884740
  18.4 16.3 %all-to-all-start = ((bf16[96,1,4,2,128]{4,0,3,1,2:T(8,128)(2,1)}), bf16[96,1,4,2,128]{4,0,3,1,2:T(8,128)(2,1)S(1)}, u32[]{:S(2)}, u32[]{:S(2)}) async-start(bf16[96,1,4,2,128]{4,0,3,1,2:T(8,128)(2,1)} %fusion.75), calls=%async_computation | async-start | bytes 393216 | tf_op jit(solution)/shard_map/all_to_all | solution.py:100
  25.0 4.9 %copy-start.5 = (bf16[96,1,4,2,128]{4,3,2,1,0:T(2,128)(2,1)S(1)}, bf16[96,1,4,2,128]{4,3,2,1,0:T(2,128)(2,1)}, u32[]{:S(2)}) copy-start(bf16[96,1,4,2,128]{4,3,2,1,0:T(2,128)(2,1)} %param.25) | copy-start | bytes 589828
  25.0 5.2 %copy-start.12 = (f32[1152]{0:T(1024)S(1)}, f32[1152]{0:T(1024)}, u32[]{:S(2)}) copy-start(f32[1152]{0:T(1024)} %param.18) | copy-start | bytes 13828
  25.0 9.3 %collective-permute-start.2 = (bf16[96,1,4,2,128]{4,3,2,1,0:T(2,128)(2,1)S(1)}, bf16[96,1,4,2,128]{4,3,2,1,0:T(2,128)(2,1)}, u32[]{:S(2)}, u32[]{:S(2)}) collective-permute-start(bf16[96,1,4,2,128]{4,3,2,1,0:T(2,128)(2,1)S(1)} %broadcast_multiply_fusion), channel_id=1, source_target_pairs={{0,8},{8,16},{16,24},{24,0},{1,9},{9,17},{17,25},{25,1},{2,10},{10... | collective-permute-start | bytes 589832 | tf_op jit(solution)/shard_map/ppermute | solution.py:163
  29.9 5.0 %copy-start.16 = (bf16[384,1152]{1,0:T(8,128)(2,1)S(1)}, bf16[384,1152]{1,0:T(8,128)(2,1)}, u32[]{:S(2)}) copy-start(bf16[384,1152]{1,0:T(8,128)(2,1)} %param.17) | copy-start | bytes 2654212
  30.4 13.7 %slice-start = ((f32[1152]{0:T(1024)}), f32[384]{0:T(512)S(1)}, s32[]{:S(2)}) async-start(f32[1152]{0:T(1024)} %param.18), calls=%async_computation.5 | async-start | bytes 4096 | tf_op jit(solution)/shard_map/slice | solution.py:108
  34.3 18.6 %collective-permute-start.3 = (bf16[96,1,4,2,128]{4,3,2,1,0:T(2,128)(2,1)}, bf16[96,1,4,2,128]{4,3,2,1,0:T(2,128)(2,1)}, u32[]{:S(2)}, u32[]{:S(2)}) collective-permute-start(bf16[96,1,4,2,128]{4,3,2,1,0:T(2,128)(2,1)} %collective-permute-done.2), channel_id=1, source_target_pairs={{0,8},{8,16},{16,24},{24,0},{1,9},{9,17},{17,25},{25,1},{2,10},{10... | collective-permute-start | bytes 589832 | tf_op jit(solution)/shard_map/ppermute | solution.py:163
  35.3 10.7 %copy-start.17 = (f32[384]{0:T(512)S(1)}, f32[384]{0:T(512)}, u32[]{:S(2)}) copy-start(f32[384]{0:T(512)} %param.20) | copy-start | bytes 4612
  46.0 12.3 %copy-start.4 = (bf16[96,1,4,2,128]{4,3,2,1,0:T(2,128)(2,1)S(1)}, bf16[96,1,4,2,128]{4,3,2,1,0:T(2,128)(2,1)}, u32[]{:S(2)}) copy-start(bf16[96,1,4,2,128]{4,3,2,1,0:T(2,128)(2,1)} %param.13) | copy-start | bytes 589828
  46.6 19.5 %copy-start.13 = (f32[96]{0:T(128)S(1)}, f32[96]{0:T(128)}, u32[]{:S(2)}) copy-start(f32[96]{0:T(128)} %param.22) | copy-start | bytes 1156
  46.6 19.5 %copy-start.14 = (f32[96]{0:T(128)S(1)}, f32[96]{0:T(128)}, u32[]{:S(2)}) copy-start(f32[96]{0:T(128)} %param.21) | copy-start | bytes 1156
  47.4 10.8 %all-to-all-start.1 = ((bf16[384,1,1,2,128]{4,3,2,1,0:T(2,128)(2,1)}), bf16[384,1,1,2,128]{4,3,2,1,0:T(2,128)(2,1)S(1)}, u32[]{:S(2)}, u32[]{:S(2)}) async-start(bf16[384,1,1,2,128]{4,3,2,1,0:T(2,128)(2,1)} %copy.39), calls=%async_computation.1 | async-start | bytes 393216 | tf_op jit(solution)/shard_map/all_to_all | solution.py:126
  52.0 93.6 %all-reduce.6.cloned.1.call-start = ((), (), s32[]{:S(2)}) async-start(), calls=%async_computation.4 | async-start | bytes 3981312 | tf_op jit(solution)/shard_map/psum | solution.py:177
  59.1 12.1 %collective-permute-start.4 = (bf16[96,1,4,2,128]{4,3,2,1,0:T(2,128)(2,1)}, bf16[96,1,4,2,128]{4,3,2,1,0:T(2,128)(2,1)S(1)}, u32[]{:S(2)}, u32[]{:S(2)}) collective-permute-start(bf16[96,1,4,2,128]{4,3,2,1,0:T(2,128)(2,1)} %collective-permute-done.3), channel_id=1, source_target_pairs={{0,8},{8,16},{16,24},{24,0},{1,9},{9,17},{17,25},{25,1},{2,10},{10... | collective-permute-start | bytes 589832 | tf_op jit(solution)/shard_map/ppermute | solution.py:163
  66.4 5.6 %collective-permute-start = (bf16[96,1,4,1,128]{4,0,3,2,1:T(8,128)(2,1)S(1)}, bf16[96,1,4,1,128]{4,0,3,2,1:T(8,128)(2,1)S(1)}, u32[]{:S(2)}, u32[]{:S(2)}) collective-permute-start(bf16[96,1,4,1,128]{4,0,3,2,1:T(8,128)(2,1)S(1)} %get-tuple-element.47), channel_id=1, source_target_pairs={{0,4},{1,5},{2,6},{3,7},{8,12},{9,13},{10,14},{11,15},{16,20},{17,... | collective-permute-start | bytes 294920 | tf_op jit(solution)/shard_map/ppermute | solution.py:17
  69.8 6.5 %collective-permute-start.1 = (bf16[96,1,4,1,128]{4,0,3,2,1:T(8,128)(2,1)S(1)}, bf16[96,1,4,1,128]{4,0,3,2,1:T(8,128)(2,1)S(1)}, u32[]{:S(2)}, u32[]{:S(2)}) collective-permute-start(bf16[96,1,4,1,128]{4,0,3,2,1:T(8,128)(2,1)S(1)} %get-tuple-element.48), channel_id=1, source_target_pairs={{4,0},{5,1},{6,2},{7,3},{12,8},{13,9},{14,10},{15,11},{20,16},{21,... | collective-permute-start | bytes 294920 | tf_op jit(solution)/shard_map/ppermute | solution.py:18
  71.2 7.9 %copy-start.6 = (bf16[384,4,2,128]{3,0,2,1:T(8,128)(2,1)}, bf16[384,4,2,128]{3,0,2,1:T(8,128)(2,1)S(1)}, u32[]{:S(2)}) copy-start(bf16[384,4,2,128]{3,0,2,1:T(8,128)(2,1)S(1)} %copy_dynamic-update-slice_fusion) | copy-start | bytes 2359300
  79.1 1.2 copy-start.10
  79.1 1.8 %copy-start.9 = (bf16[864,1,4,2,128]{4,0,3,2,1:T(8,128)(2,1)}, bf16[864,1,4,2,128]{4,0,3,2,1:T(8,128)(2,1)S(1)}, u32[]{:S(2)}) copy-start(bf16[864,1,4,2,128]{4,0,3,2,1:T(8,128)(2,1)S(1)} %get-tuple-element.24) | copy-start | bytes 5308420
  80.3 1.1 copy-start.7
  80.7 2.0 %copy-start.2 = (bf16[864,1,4,2,128]{4,0,3,2,1:T(8,128)(2,1)}, bf16[864,1,4,2,128]{4,0,3,2,1:T(8,128)(2,1)S(1)}, u32[]{:S(2)}) copy-start(bf16[864,1,4,2,128]{4,0,3,2,1:T(8,128)(2,1)S(1)} %slice_dynamic-update-slice_fusion) | copy-start | bytes 5308420
  83.8 1.3 copy-start.1
  85.1 64.4 %reduce-scatter.2.cloned.1.call-start = ((), (), s32[]{:S(2)}) async-start(), calls=%async_computation.3 | async-start | bytes 983040 | tf_op jit(solution)/shard_map/reduce_scatter | solution.py:143
  85.3 2.8 %copy-start.8 = (bf16[1,3,3,96,384]{4,3,2,1,0:T(8,128)(2,1)S(1)}, bf16[1,3,3,96,384]{4,3,2,1,0:T(8,128)(2,1)}, u32[]{:S(2)}) copy-start(bf16[1,3,3,96,384]{4,3,2,1,0:T(8,128)(2,1)} %get-tuple-element.22) | copy-start | bytes 1990660
  85.3 2.8 %copy-start.11 = (bf16[864,1,4,2,128]{4,0,3,2,1:T(8,128)(2,1)S(1)}, bf16[864,1,4,2,128]{4,0,3,2,1:T(8,128)(2,1)}, u32[]{:S(2)}) copy-start(bf16[864,1,4,2,128]{4,0,3,2,1:T(8,128)(2,1)} %copy-done.10) | copy-start | bytes 5308420
  88.2 1.6 copy-start.3
  91.7 57.8 %copy-start.15 = (f32[96]{0:T(128)S(1)}, f32[96]{0:T(128)}, u32[]{:S(2)}) copy-start(f32[96]{0:T(128)} %param.24) | copy-start | bytes 1156
Sparse Core Ops, SparseCore 0:
  85.2 60.2 all-reduce.5
Sparse Core Ops, SparseCore 1:
  91.8 22.0 reduce-scatter.1
